TPU v7x, 256 devices: a whole 4x4x8 slice. The times are simulated.
256 devices in a mesh: row: 16 (over y, z_hi, core), col: 16 (over z_lo, x).
Axes of the slice: x: 4, y: 4, z: 8 (z_hi: 2, z_lo: 4; z = z_hi * 4 + z_lo), core: 2. Of those that a mesh axis runs over, the one named last changes fastest.
Arguments:
- queries: bfloat16 [32, 16, 128, 2048], P('row', 'col'), may hold values from -70 to 70
- fine_keys: bfloat16 [32, 16, 128, 2048], P('row', 'col'), may hold values from -4 to 4
- fine_values: bfloat16 [32, 16, 128, 2048], P('row', 'col'), may hold values from -6 to 6
- keep_flags: int32 [32, 16, 9], P('row', 'col'), may hold values 0 or 1
- coarse_keys: bfloat16 [2048, 2048], P('col'), may hold values from -6 to 6
- coarse_values: bfloat16 [2048, 2048], P('col'), may hold values from -6 to 6
Outputs:
- attended: bfloat16 [32, 16, 128, 2048], P('row', 'col')
All inputs are finite; a program needn't handle non-finite values. No bound on the sum of `keep_flags` on one device may be relied on, other than what follows from the above.
Results may differ from a plain program's by a relative error of at most 0.0035.
Values may be sent and summed in bfloat16 or wider, within the bound.
A program may use at most 128 MiB of HBM per device.

v0:
```python
import jax
import jax.numpy as jnp
from jax import lax
from jax.sharding import PartitionSpec as P

HEADS = 16
HEAD_DIM = 128


def padded_2(cells, sides, width):
    for axis, dim in sides:
        count = lax.axis_size(axis)
        ends = count - 1
        head = lax.slice_in_dim(cells, 0, width, axis=dim)
        tail = lax.slice_in_dim(cells, cells.shape[dim] - width, cells.shape[dim], axis=dim)
        cells = jnp.concatenate(
            [
                lax.ppermute(tail, axis, [(i, (i + 1) % count) for i in range(ends)]),
                cells,
                lax.ppermute(head, axis, [((i + 1) % count, i) for i in range(ends)]),
            ],
            axis=dim,
        )
    return cells


def body(queries, fine_keys, fine_values, keep_flags, coarse_keys, coarse_values):
    rows_tiles, cols_tiles, tile_len, model_width = queries.shape
    tile_count = rows_tiles * cols_tiles
    scale = HEAD_DIM ** (-0.5)
    stacked = jnp.stack((fine_keys, fine_values), 0)
    padded = padded_2(stacked, (("row", 1), ("col", 2)), 1)
    far_keys, far_values = (
        lax.all_gather(coarse_keys, "col", axis=0, tiled=True),
        lax.all_gather(coarse_values, "col", axis=0, tiled=True),
    )
    row_base = lax.axis_index("row") * rows_tiles
    col_base = lax.axis_index("col") * cols_tiles
    rows_total = rows_tiles * lax.axis_size("row")
    cols_total = cols_tiles * lax.axis_size("col")
    windows = []
    usable = []
    for tile_row in range(rows_tiles):
        pieces = []
        kept_list = []
        for row_step in range(3):
            for col_step in range(3):
                pieces.append(padded[:, tile_row + row_step, col_step])
                grid_row = row_base + tile_row + row_step - 1
                grid_col = col_base + 0 + col_step - 1
                inside = (
                    (grid_row >= 0)
                    & (grid_row < rows_total)
                    & (grid_col >= 0)
                    & (grid_col < cols_total)
                )
                kept_here = (keep_flags[tile_row, 0, row_step * 3 + col_step] > 0) | (
                    row_step == 1 and col_step == 1
                )
                kept_list.append(inside & kept_here)
        windows.append(jnp.concatenate(pieces, axis=1))
        usable.append(jnp.stack(kept_list))
    window_kv = jnp.stack(windows, 1)
    window_ok = jnp.repeat(jnp.stack(usable), tile_len, axis=1)
    query_flat = queries.reshape(tile_count, tile_len, model_width)

    def one_head(head):
        begin_at = head * HEAD_DIM
        query_head = lax.dynamic_slice_in_dim(query_flat, begin_at, HEAD_DIM, 2)
        near_keys = lax.dynamic_slice_in_dim(window_kv[0], begin_at, HEAD_DIM, 2)
        near_values = lax.dynamic_slice_in_dim(window_kv[1], begin_at, HEAD_DIM, 2)
        far_key_head = lax.dynamic_slice_in_dim(far_keys, begin_at, HEAD_DIM, 1)
        far_value_head = lax.dynamic_slice_in_dim(far_values, begin_at, HEAD_DIM, 1)
        near_scores = (
            jnp.einsum("tqd,tkd->tqk", query_head, near_keys, preferred_element_type=jnp.float32)
            * scale
        )
        near_scores = jnp.where(window_ok[:, None, :], near_scores, -jnp.inf)
        far_scores = (
            jnp.einsum("tqd,kd->tqk", query_head, far_key_head, preferred_element_type=jnp.float32)
            * scale
        )
        largest = jnp.maximum(jnp.max(near_scores, -1), jnp.max(far_scores, -1))[..., None]
        near_probs = jnp.exp(near_scores - largest)
        far_probs = jnp.exp(far_scores - largest)
        total = jnp.sum(near_probs, -1) + jnp.sum(far_probs, -1)
        mixed = jnp.einsum(
            "tqk,tkd->tqd",
            near_probs.astype(jnp.bfloat16),
            near_values,
            preferred_element_type=jnp.float32,
        )
        mixed = mixed + jnp.einsum(
            "tqk,kd->tqd",
            far_probs.astype(jnp.bfloat16),
            far_value_head,
            preferred_element_type=jnp.float32,
        )
        return mixed / total[..., None]

    result = lax.map(one_head, jnp.arange(HEADS))
    result = jnp.transpose(result, (1, 2, 0, 3)).reshape(
        rows_tiles, cols_tiles, tile_len, model_width
    )
    return result.astype(jnp.bfloat16)


def solution(mesh):
    placed = (
        P("row", "col", None, None),
        P("row", "col", None, None),
        P("row", "col", None, None),
        P("row", "col", None),
        P("col", None),
        P("col", None),
    )
    return jax.shard_map(
        body, mesh=mesh, in_specs=placed, out_specs=P("row", "col", None, None), check_vma=False
    )
```

profile of v0, /device:TPU:89, one launch (start us, length us, event | category | flops | bytes accessed | tf_op | source)
XLA Modules:
  0.0 578.8 jit_solution(1291833222597962540)
XLA Ops:
  9.7 7.6 %collective-permute-start = (bf16[2,1,1,128,2048]{4,3,0,2,1:T(8,128)(2,1)S(1)}, bf16[2,1,1,128,2048]{4,3,0,2,1:T(8,128)(2,1)S(1)}, u32[]{:S(2)}, u32[]{:S(2)}) collective-permute-start(bf16[2,1,1,128,2048]{4,3,0,2,1:T(8,128)(2,1)S(1)} %get-tuple-element.97), channel_id=1, source_target_pairs={{0,16},{16,32},{32,48},{48,64},{64,80},{80,96},{96,112},{112,128},... | collective-permute-start | bytes 3145736 | tf_op jit(solution)/shard_map/ppermute | solution.py:18
  19.2 87.9 %collective-permute-done = bf16[2,1,1,128,2048]{4,3,0,2,1:T(8,128)(2,1)S(1)} collective-permute-done((bf16[2,1,1,128,2048]{4,3,0,2,1:T(8,128)(2,1)S(1)}, bf16[2,1,1,128,2048]{4,3,0,2,1:T(8,128)(2,1)S(1)}, u32[]{:S(2)}, u32[]{:S(2)}) %collective-permute-start) | collective-permute-done | bytes 1048608 | tf_op jit(solution)/shard_map/ppermute | solution.py:18
  113.6 5.5 collective-permute-start.3
  130.3 112.3 %collective-permute-done.2 = bf16[2,4,1,128,2048]{4,3,0,2,1:T(8,128)(2,1)} collective-permute-done((bf16[2,4,1,128,2048]{4,3,0,2,1:T(8,128)(2,1)}, bf16[2,4,1,128,2048]{4,3,0,2,1:T(8,128)(2,1)}, u32[]{:S(2)}, u32[]{:S(2)}) %collective-permute-start.2) | collective-permute-done | bytes 4194336 | tf_op jit(solution)/shard_map/ppermute | solution.py:18
  245.2 8.8 %collective-permute-done.3 = bf16[2,4,1,128,2048]{4,3,0,2,1:T(8,128)(2,1)} collective-permute-done((bf16[2,4,1,128,2048]{4,3,0,2,1:T(8,128)(2,1)}, bf16[2,4,1,128,2048]{4,3,0,2,1:T(8,128)(2,1)}, u32[]{:S(2)}, u32[]{:S(2)}) %collective-permute-start.3) | collective-permute-done | bytes 4194336 | tf_op jit(solution)/shard_map/ppermute | solution.py:20
  264.8 7.7 %pad_maximum_fusion = bf16[2,2,1152,2048]{3,2,1,0:T(8,128)(2,1)} fusion(bf16[2,1,1152,2048]{3,2,1,0:T(8,128)(2,1)S(1)} %bitcast.140, bf16[2,1,1152,2048]{3,2,1,0:T(8,128)(2,1)S(1)} %bitcast.141), kind=kLoop, calls=%fused_computation.33 | loop fusion | flops 9437184 | bytes 37748736 | tf_op jit(solution)/shard_map/stack | solution.py:63
  272.5 54.6 %all-gather.5.cloned.1.call-done = bf16[2048,2048]{1,0:T(8,128)(2,1)} async-done(((bf16[128,2048]{1,0:T(8,128)(2,1)}), bf16[2048,2048]{1,0:T(8,128)(2,1)}) %all-gather.5.cloned.1.call-update) | async-done | bytes 8388624 | tf_op jit(solution)/shard_map/all_gather | solution.py:35
  327.1 242.9 %while.11 = (s32[]{:T(128)}, bf16[16,2,128,128]{3,2,1,0:T(8,128)(2,1)S(1)}, s32[16]{0:T(128)S(1)}, bf16[2,128,2048]{2,1,0:T(8,128)(2,1)}, bf16[2,2,1152,2048]{3,...) while((s32[]{:T(128)}, ...), condition=%wide.region_5.6_spmd.clone, body=%wide.region_0.5_spmd.clone.sunk | while | flops 424705536 | bytes 50360780 | solution.py:101
  328.4 8.1 %fusion.62 = (bf16[1,2,1152,2048]{3,2,1,0:T(8,128)(2,1)S(1)}, bf16[1,2,1152,2048]{3,2,1,0:T(8,128)(2,1)S(1)}) fusion(bf16[2,2,1152,2048]{3,2,1,0:T(8,128)(2,1)} %get-tuple-element.208), kind=kLoop, calls=%fused_computation.67.clone.1 | loop fusion | bytes 37748736 | tf_op jit(solution)/shard_map/while/body/eval_jaxpr/slice | solution.py:71
  343.6 8.1 %fusion.62 = (bf16[1,2,1152,2048]{3,2,1,0:T(8,128)(2,1)S(1)}, bf16[1,2,1152,2048]{3,2,1,0:T(8,128)(2,1)S(1)}) fusion(bf16[2,2,1152,2048]{3,2,1,0:T(8,128)(2,1)} %get-tuple-element.208), kind=kLoop, calls=%fused_computation.67.clone.1 | loop fusion | bytes 37748736 | tf_op jit(solution)/shard_map/while/body/eval_jaxpr/slice | solution.py:71
  358.8 8.1 %fusion.62 = (bf16[1,2,1152,2048]{3,2,1,0:T(8,128)(2,1)S(1)}, bf16[1,2,1152,2048]{3,2,1,0:T(8,128)(2,1)S(1)}) fusion(bf16[2,2,1152,2048]{3,2,1,0:T(8,128)(2,1)} %get-tuple-element.208), kind=kLoop, calls=%fused_computation.67.clone.1 | loop fusion | bytes 37748736 | tf_op jit(solution)/shard_map/while/body/eval_jaxpr/slice | solution.py:71
  374.0 8.1 %fusion.62 = (bf16[1,2,1152,2048]{3,2,1,0:T(8,128)(2,1)S(1)}, bf16[1,2,1152,2048]{3,2,1,0:T(8,128)(2,1)S(1)}) fusion(bf16[2,2,1152,2048]{3,2,1,0:T(8,128)(2,1)} %get-tuple-element.208), kind=kLoop, calls=%fused_computation.67.clone.1 | loop fusion | bytes 37748736 | tf_op jit(solution)/shard_map/while/body/eval_jaxpr/slice | solution.py:71
  389.1 8.1 %fusion.62 = (bf16[1,2,1152,2048]{3,2,1,0:T(8,128)(2,1)S(1)}, bf16[1,2,1152,2048]{3,2,1,0:T(8,128)(2,1)S(1)}) fusion(bf16[2,2,1152,2048]{3,2,1,0:T(8,128)(2,1)} %get-tuple-element.208), kind=kLoop, calls=%fused_computation.67.clone.1 | loop fusion | bytes 37748736 | tf_op jit(solution)/shard_map/while/body/eval_jaxpr/slice | solution.py:71
  404.3 8.1 %fusion.62 = (bf16[1,2,1152,2048]{3,2,1,0:T(8,128)(2,1)S(1)}, bf16[1,2,1152,2048]{3,2,1,0:T(8,128)(2,1)S(1)}) fusion(bf16[2,2,1152,2048]{3,2,1,0:T(8,128)(2,1)} %get-tuple-element.208), kind=kLoop, calls=%fused_computation.67.clone.1 | loop fusion | bytes 37748736 | tf_op jit(solution)/shard_map/while/body/eval_jaxpr/slice | solution.py:71
  419.5 8.1 %fusion.62 = (bf16[1,2,1152,2048]{3,2,1,0:T(8,128)(2,1)S(1)}, bf16[1,2,1152,2048]{3,2,1,0:T(8,128)(2,1)S(1)}) fusion(bf16[2,2,1152,2048]{3,2,1,0:T(8,128)(2,1)} %get-tuple-element.208), kind=kLoop, calls=%fused_computation.67.clone.1 | loop fusion | bytes 37748736 | tf_op jit(solution)/shard_map/while/body/eval_jaxpr/slice | solution.py:71
  434.7 8.1 %fusion.62 = (bf16[1,2,1152,2048]{3,2,1,0:T(8,128)(2,1)S(1)}, bf16[1,2,1152,2048]{3,2,1,0:T(8,128)(2,1)S(1)}) fusion(bf16[2,2,1152,2048]{3,2,1,0:T(8,128)(2,1)} %get-tuple-element.208), kind=kLoop, calls=%fused_computation.67.clone.1 | loop fusion | bytes 37748736 | tf_op jit(solution)/shard_map/while/body/eval_jaxpr/slice | solution.py:71
  449.8 8.1 %fusion.62 = (bf16[1,2,1152,2048]{3,2,1,0:T(8,128)(2,1)S(1)}, bf16[1,2,1152,2048]{3,2,1,0:T(8,128)(2,1)S(1)}) fusion(bf16[2,2,1152,2048]{3,2,1,0:T(8,128)(2,1)} %get-tuple-element.208), kind=kLoop, calls=%fused_computation.67.clone.1 | loop fusion | bytes 37748736 | tf_op jit(solution)/shard_map/while/body/eval_jaxpr/slice | solution.py:71
  465.0 8.1 %fusion.62 = (bf16[1,2,1152,2048]{3,2,1,0:T(8,128)(2,1)S(1)}, bf16[1,2,1152,2048]{3,2,1,0:T(8,128)(2,1)S(1)}) fusion(bf16[2,2,1152,2048]{3,2,1,0:T(8,128)(2,1)} %get-tuple-element.208), kind=kLoop, calls=%fused_computation.67.clone.1 | loop fusion | bytes 37748736 | tf_op jit(solution)/shard_map/while/body/eval_jaxpr/slice | solution.py:71
  480.2 8.1 %fusion.62 = (bf16[1,2,1152,2048]{3,2,1,0:T(8,128)(2,1)S(1)}, bf16[1,2,1152,2048]{3,2,1,0:T(8,128)(2,1)S(1)}) fusion(bf16[2,2,1152,2048]{3,2,1,0:T(8,128)(2,1)} %get-tuple-element.208), kind=kLoop, calls=%fused_computation.67.clone.1 | loop fusion | bytes 37748736 | tf_op jit(solution)/shard_map/while/body/eval_jaxpr/slice | solution.py:71
  495.4 8.1 %fusion.62 = (bf16[1,2,1152,2048]{3,2,1,0:T(8,128)(2,1)S(1)}, bf16[1,2,1152,2048]{3,2,1,0:T(8,128)(2,1)S(1)}) fusion(bf16[2,2,1152,2048]{3,2,1,0:T(8,128)(2,1)} %get-tuple-element.208), kind=kLoop, calls=%fused_computation.67.clone.1 | loop fusion | bytes 37748736 | tf_op jit(solution)/shard_map/while/body/eval_jaxpr/slice | solution.py:71
  510.6 8.1 %fusion.62 = (bf16[1,2,1152,2048]{3,2,1,0:T(8,128)(2,1)S(1)}, bf16[1,2,1152,2048]{3,2,1,0:T(8,128)(2,1)S(1)}) fusion(bf16[2,2,1152,2048]{3,2,1,0:T(8,128)(2,1)} %get-tuple-element.208), kind=kLoop, calls=%fused_computation.67.clone.1 | loop fusion | bytes 37748736 | tf_op jit(solution)/shard_map/while/body/eval_jaxpr/slice | solution.py:71
  525.8 8.1 %fusion.62 = (bf16[1,2,1152,2048]{3,2,1,0:T(8,128)(2,1)S(1)}, bf16[1,2,1152,2048]{3,2,1,0:T(8,128)(2,1)S(1)}) fusion(bf16[2,2,1152,2048]{3,2,1,0:T(8,128)(2,1)} %get-tuple-element.208), kind=kLoop, calls=%fused_computation.67.clone.1 | loop fusion | bytes 37748736 | tf_op jit(solution)/shard_map/while/body/eval_jaxpr/slice | solution.py:71
  540.9 8.1 %fusion.62 = (bf16[1,2,1152,2048]{3,2,1,0:T(8,128)(2,1)S(1)}, bf16[1,2,1152,2048]{3,2,1,0:T(8,128)(2,1)S(1)}) fusion(bf16[2,2,1152,2048]{3,2,1,0:T(8,128)(2,1)} %get-tuple-element.208), kind=kLoop, calls=%fused_computation.67.clone.1 | loop fusion | bytes 37748736 | tf_op jit(solution)/shard_map/while/body/eval_jaxpr/slice | solution.py:71
  556.1 8.1 %fusion.62 = (bf16[1,2,1152,2048]{3,2,1,0:T(8,128)(2,1)S(1)}, bf16[1,2,1152,2048]{3,2,1,0:T(8,128)(2,1)S(1)}) fusion(bf16[2,2,1152,2048]{3,2,1,0:T(8,128)(2,1)} %get-tuple-element.208), kind=kLoop, calls=%fused_computation.67.clone.1 | loop fusion | bytes 37748736 | tf_op jit(solution)/shard_map/while/body/eval_jaxpr/slice | solution.py:71
  (212 shorter events, 129.4 us)
Async XLA Ops:
  6.5 112.6 %copy-start.2 = (s32[2,1,9]{2,1,0:T(1,128)S(1)}, s32[2,1,9]{2,1,0:T(1,128)}, u32[]{:S(2)}) copy-start(s32[2,1,9]{2,1,0:T(1,128)} %param.11) | copy-start | bytes 220
  6.5 266.0 %all-gather.3.cloned.1.call-start = ((), (), s32[]{:S(2)}) async-start(), calls=%async_computation | async-start | bytes 8912896 | tf_op jit(solution)/shard_map/all_gather | solution.py:34
  7.3 319.9 %all-gather.5.cloned.1.call-start = ((), (), s32[]{:S(2)}) async-start(), calls=%async_computation.1 | async-start | bytes 8912896 | tf_op jit(solution)/shard_map/all_gather | solution.py:35
  9.7 97.5 %collective-permute-start = (bf16[2,1,1,128,2048]{4,3,0,2,1:T(8,128)(2,1)S(1)}, bf16[2,1,1,128,2048]{4,3,0,2,1:T(8,128)(2,1)S(1)}, u32[]{:S(2)}, u32[]{:S(2)}) collective-permute-start(bf16[2,1,1,128,2048]{4,3,0,2,1:T(8,128)(2,1)S(1)} %get-tuple-element.97), channel_id=1, source_target_pairs={{0,16},{16,32},{32,48},{48,64},{64,80},{80,96},{96,112},{112,128},... | collective-permute-start | bytes 3145736 | tf_op jit(solution)/shard_map/ppermute | solution.py:18
  17.3 89.9 %collective-permute-start.1 = (bf16[2,1,1,128,2048]{4,3,0,2,1:T(8,128)(2,1)S(1)}, bf16[2,1,1,128,2048]{4,3,0,2,1:T(8,128)(2,1)S(1)}, u32[]{:S(2)}, u32[]{:S(2)}) collective-permute-start(bf16[2,1,1,128,2048]{4,3,0,2,1:T(8,128)(2,1)S(1)} %get-tuple-element.98), channel_id=1, source_target_pairs={{16,0},{32,16},{48,32},{64,48},{80,64},{96,80},{112,96},{128,112},... | collective-permute-start | bytes 3145736 | tf_op jit(solution)/shard_map/ppermute | solution.py:20
  107.2 1.1 copy-start
  111.7 130.9 %collective-permute-start.2 = (bf16[2,4,1,128,2048]{4,3,0,2,1:T(8,128)(2,1)}, bf16[2,4,1,128,2048]{4,3,0,2,1:T(8,128)(2,1)}, u32[]{:S(2)}, u32[]{:S(2)}) collective-permute-start(bf16[2,4,1,128,2048]{4,3,0,2,1:T(8,128)(2,1)} %pad_maximum_fusion.1), channel_id=1, source_target_pairs={{0,1},{1,2},{2,3},{3,4},{4,5},{5,6},{6,7},{7,8},{8,9},{9,10},{10,1... | collective-permute-start | bytes 12582920 | tf_op jit(solution)/shard_map/ppermute | solution.py:18
  113.6 140.4 %collective-permute-start.3 = (bf16[2,4,1,128,2048]{4,3,0,2,1:T(8,128)(2,1)}, bf16[2,4,1,128,2048]{4,3,0,2,1:T(8,128)(2,1)}, u32[]{:S(2)}, u32[]{:S(2)}) collective-permute-start(bf16[2,4,1,128,2048]{4,3,0,2,1:T(8,128)(2,1)} %pad_maximum_fusion.1), channel_id=1, source_target_pairs={{1,0},{2,1},{3,2},{4,3},{5,4},{6,5},{7,6},{8,7},{9,8},{10,9},{11,1... | collective-permute-start | bytes 12582920 | tf_op jit(solution)/shard_map/ppermute | solution.py:20
  264.8 62.3 %copy-start.1 = (bf16[16,2,128,128]{3,2,1,0:T(8,128)(2,1)S(1)}, bf16[16,2,128,128]{3,2,1,0:T(8,128)(2,1)}, u32[]{:S(2)}) copy-start(bf16[16,2,128,128]{3,2,1,0:T(8,128)(2,1)} %custom-call.2) | copy-start | bytes 3145732
Sparse Core Ops, SparseCore 0:
  9.1 177.1 all-gather.2
  188.1 138.9 all-gather.4
where the time goes:
time: 582 us; the launch traced here: 579 us
  waiting for transfers between devices  265 us (46%)
  local copies, waits for them, and re-layouts  158 us (27%)
  matrix products  78.3 us (13%)
  other arithmetic  25.5 us (4%)
  between operations  23.8 us (4%)
  starting transfers between devices  16.9 us (3%)
  loops' own time  11.2 us (2%)
    ppermute x2, waiting for transfers between devices, padded_2(): lax.ppermute(tail, axis, [(i, (i + 1) % count) for i in range(ends)])  200 us
    slice x16, local copies, waits for them, and re-layouts, one_head(): near_values = lax.dynamic_slice_in_dim(window_kv[1], begin_at, HEAD_DIM, 2)  130 us
    all_gather x1, waiting for transfers between devices, body(): lax.all_gather(coarse_values, 'col', axis=0, tiled=True)  54.6 us
    dot_general x16, matrix products, one_head(): jnp.einsum('tqd,kd->tqk', query_head, far_key_head, preferred_element_typ...  25.6 us
    dot_general x16, matrix products, one_head(): jnp.einsum('tqk,kd->tqd', far_probs.astype(jnp.bfloat16), far_value_head,...  25 us
    dot_general x16, matrix products, one_head(): jnp.einsum('tqd,tkd->tqk', query_head, near_keys, preferred_element_type=...  20.5 us
    reduce_sum x32, other arithmetic, one_head(): total = jnp.sum(near_probs, -1) + jnp.sum(far_probs, -1)  12.4 us
  transfers between devices with their start and end apart: 6, of which 4 were waited for; matrix products, arithmetic and copies ran while one was open for 5% of the time, Pallas kernels for 0%

commit v1 on v0

--- a/solution.py
+++ b/solution.py
@@ -32,7 +32,9 @@
     padded = padded_2(stacked, (("row", 1), ("col", 2)), 1)
     far_keys, far_values = (
         lax.all_gather(coarse_keys, "col", axis=0, tiled=True),
-        lax.all_gather(coarse_values, "col", axis=0, tiled=True),
+        jnp.concatenate(
+            lax.all_to_all(jnp.stack([coarse_values] * lax.axis_size("col")), "col", 0, 0), axis=0
+        ),
     )
     row_base = lax.axis_index("row") * rows_tiles
     col_base = lax.axis_index("col") * cols_tiles

time: 582 us -> 698 us (1.20)
  the two profiles are of different devices: /device:TPU:89 before, /device:TPU:46 now
where the time goes in v1:
time: 698 us; the launch traced here: 695 us
  waiting for transfers between devices  369 us (53%)
  local copies, waits for them, and re-layouts  164 us (23%)
  matrix products  78.3 us (11%)
  other arithmetic  25 us (4%)
  starting transfers between devices  24.8 us (4%)
  between operations  23.8 us (3%)
  loops' own time  11.2 us (2%)
    ppermute x2, waiting for transfers between devices, padded_2(): lax.ppermute(tail, axis, [(i, (i + 1) % count) for i in range(ends)])  365 us
    slice x16, local copies, waits for them, and re-layouts, one_head(): near_values = lax.dynamic_slice_in_dim(window_kv[1], begin_at, HEAD_DIM, 2)  130 us
    dot_general x16, matrix products, one_head(): jnp.einsum('tqd,kd->tqk', query_head, far_key_head, preferred_element_typ...  25.7 us
    dot_general x16, matrix products, one_head(): jnp.einsum('tqk,kd->tqd', far_probs.astype(jnp.bfloat16), far_value_head,...  25 us
    dot_general x16, matrix products, one_head(): jnp.einsum('tqd,tkd->tqk', query_head, near_keys, preferred_element_type=...  20.5 us
  transfers between devices with their start and end apart: 6, of which 3 were waited for; matrix products, arithmetic and copies ran while one was open for 4% of the time, Pallas kernels for 0%

profile of v1, /device:TPU:46, one launch (start us, length us, event | category | flops | bytes accessed | tf_op | source)
XLA Modules:
  0.0 695.3 jit_solution(11791256573808271282)
XLA Ops:
  6.5 5.5 stack.135
  12.0 8.5 %all-to-all-start = ((bf16[16,128,2048]{2,1,0:T(8,128)(2,1)}), bf16[16,128,2048]{2,1,0:T(8,128)(2,1)}, u32[]{:S(2)}, u32[]{:S(2)}) async-start(bf16[16,128,2048]{2,1,0:T(8,128)(2,1)} %stack.135), calls=%async_computation | async-start | bytes 16777216 | tf_op jit(solution)/shard_map/all_to_all | solution.py:36
  24.6 8.4 %collective-permute-start.1 = (bf16[2,1,1,128,2048]{4,3,0,2,1:T(8,128)(2,1)S(1)}, bf16[2,1,1,128,2048]{4,3,0,2,1:T(8,128)(2,1)S(1)}, u32[]{:S(2)}, u32[]{:S(2)}) collective-permute-start(bf16[2,1,1,128,2048]{4,3,0,2,1:T(8,128)(2,1)S(1)} %get-tuple-element.98), channel_id=1, source_target_pairs={{16,0},{32,16},{48,32},{64,48},{80,64},{96,80},{112,96},{128,112},... | collective-permute-start | bytes 3145736 | tf_op jit(solution)/shard_map/ppermute | solution.py:20
  33.0 158.3 %collective-permute-done = bf16[2,1,1,128,2048]{4,3,0,2,1:T(8,128)(2,1)S(1)} collective-permute-done((bf16[2,1,1,128,2048]{4,3,0,2,1:T(8,128)(2,1)S(1)}, bf16[2,1,1,128,2048]{4,3,0,2,1:T(8,128)(2,1)S(1)}, u32[]{:S(2)}, u32[]{:S(2)}) %collective-permute-start) | collective-permute-done | bytes 1048608 | tf_op jit(solution)/shard_map/ppermute | solution.py:18
  197.8 3.9 collective-permute-start.3
  212.9 206.5 %collective-permute-done.2 = bf16[2,4,1,128,2048]{4,3,0,2,1:T(8,128)(2,1)} collective-permute-done((bf16[2,4,1,128,2048]{4,3,0,2,1:T(8,128)(2,1)}, bf16[2,4,1,128,2048]{4,3,0,2,1:T(8,128)(2,1)}, u32[]{:S(2)}, u32[]{:S(2)}) %collective-permute-start.2) | collective-permute-done | bytes 4194336 | tf_op jit(solution)/shard_map/ppermute | solution.py:18
  436.1 7.7 %pad_maximum_fusion = bf16[2,2,1152,2048]{3,2,1,0:T(8,128)(2,1)} fusion(bf16[2,1,1152,2048]{3,2,1,0:T(8,128)(2,1)S(1)} %bitcast.141, bf16[2,1,1152,2048]{3,2,1,0:T(8,128)(2,1)S(1)} %bitcast.142), kind=kLoop, calls=%fused_computation.33 | loop fusion | flops 9437184 | bytes 37748736 | tf_op jit(solution)/shard_map/stack | solution.py:65
  443.8 242.7 %while.11 = (s32[]{:T(128)}, bf16[16,2,128,128]{3,2,1,0:T(8,128)(2,1)S(1)}, s32[16]{0:T(128)S(1)}, bf16[2,128,2048]{2,1,0:T(8,128)(2,1)}, bf16[2,2,1152,2048]{3,...) while((s32[]{:T(128)}, ...), condition=%wide.region_5.6_spmd.clone, body=%wide.region_0.5_spmd.clone.sunk | while | flops 424705536 | bytes 50360780 | solution.py:103
  445.1 8.1 %fusion.62 = (bf16[1,2,1152,2048]{3,2,1,0:T(8,128)(2,1)S(1)}, bf16[1,2,1152,2048]{3,2,1,0:T(8,128)(2,1)S(1)}) fusion(bf16[2,2,1152,2048]{3,2,1,0:T(8,128)(2,1)} %get-tuple-element.208), kind=kLoop, calls=%fused_computation.67.clone.1 | loop fusion | bytes 37748736 | tf_op jit(solution)/shard_map/while/body/eval_jaxpr/slice | solution.py:73
  460.2 8.1 %fusion.62 = (bf16[1,2,1152,2048]{3,2,1,0:T(8,128)(2,1)S(1)}, bf16[1,2,1152,2048]{3,2,1,0:T(8,128)(2,1)S(1)}) fusion(bf16[2,2,1152,2048]{3,2,1,0:T(8,128)(2,1)} %get-tuple-element.208), kind=kLoop, calls=%fused_computation.67.clone.1 | loop fusion | bytes 37748736 | tf_op jit(solution)/shard_map/while/body/eval_jaxpr/slice | solution.py:73
  475.4 8.1 %fusion.62 = (bf16[1,2,1152,2048]{3,2,1,0:T(8,128)(2,1)S(1)}, bf16[1,2,1152,2048]{3,2,1,0:T(8,128)(2,1)S(1)}) fusion(bf16[2,2,1152,2048]{3,2,1,0:T(8,128)(2,1)} %get-tuple-element.208), kind=kLoop, calls=%fused_computation.67.clone.1 | loop fusion | bytes 37748736 | tf_op jit(solution)/shard_map/while/body/eval_jaxpr/slice | solution.py:73
  490.6 8.1 %fusion.62 = (bf16[1,2,1152,2048]{3,2,1,0:T(8,128)(2,1)S(1)}, bf16[1,2,1152,2048]{3,2,1,0:T(8,128)(2,1)S(1)}) fusion(bf16[2,2,1152,2048]{3,2,1,0:T(8,128)(2,1)} %get-tuple-element.208), kind=kLoop, calls=%fused_computation.67.clone.1 | loop fusion | bytes 37748736 | tf_op jit(solution)/shard_map/while/body/eval_jaxpr/slice | solution.py:73
  505.7 8.1 %fusion.62 = (bf16[1,2,1152,2048]{3,2,1,0:T(8,128)(2,1)S(1)}, bf16[1,2,1152,2048]{3,2,1,0:T(8,128)(2,1)S(1)}) fusion(bf16[2,2,1152,2048]{3,2,1,0:T(8,128)(2,1)} %get-tuple-element.208), kind=kLoop, calls=%fused_computation.67.clone.1 | loop fusion | bytes 37748736 | tf_op jit(solution)/shard_map/while/body/eval_jaxpr/slice | solution.py:73
  520.9 8.1 %fusion.62 = (bf16[1,2,1152,2048]{3,2,1,0:T(8,128)(2,1)S(1)}, bf16[1,2,1152,2048]{3,2,1,0:T(8,128)(2,1)S(1)}) fusion(bf16[2,2,1152,2048]{3,2,1,0:T(8,128)(2,1)} %get-tuple-element.208), kind=kLoop, calls=%fused_computation.67.clone.1 | loop fusion | bytes 37748736 | tf_op jit(solution)/shard_map/while/body/eval_jaxpr/slice | solution.py:73
  536.1 8.1 %fusion.62 = (bf16[1,2,1152,2048]{3,2,1,0:T(8,128)(2,1)S(1)}, bf16[1,2,1152,2048]{3,2,1,0:T(8,128)(2,1)S(1)}) fusion(bf16[2,2,1152,2048]{3,2,1,0:T(8,128)(2,1)} %get-tuple-element.208), kind=kLoop, calls=%fused_computation.67.clone.1 | loop fusion | bytes 37748736 | tf_op jit(solution)/shard_map/while/body/eval_jaxpr/slice | solution.py:73
  551.2 8.1 %fusion.62 = (bf16[1,2,1152,2048]{3,2,1,0:T(8,128)(2,1)S(1)}, bf16[1,2,1152,2048]{3,2,1,0:T(8,128)(2,1)S(1)}) fusion(bf16[2,2,1152,2048]{3,2,1,0:T(8,128)(2,1)} %get-tuple-element.208), kind=kLoop, calls=%fused_computation.67.clone.1 | loop fusion | bytes 37748736 | tf_op jit(solution)/shard_map/while/body/eval_jaxpr/slice | solution.py:73
  566.4 8.1 %fusion.62 = (bf16[1,2,1152,2048]{3,2,1,0:T(8,128)(2,1)S(1)}, bf16[1,2,1152,2048]{3,2,1,0:T(8,128)(2,1)S(1)}) fusion(bf16[2,2,1152,2048]{3,2,1,0:T(8,128)(2,1)} %get-tuple-element.208), kind=kLoop, calls=%fused_computation.67.clone.1 | loop fusion | bytes 37748736 | tf_op jit(solution)/shard_map/while/body/eval_jaxpr/slice | solution.py:73
  581.6 8.1 %fusion.62 = (bf16[1,2,1152,2048]{3,2,1,0:T(8,128)(2,1)S(1)}, bf16[1,2,1152,2048]{3,2,1,0:T(8,128)(2,1)S(1)}) fusion(bf16[2,2,1152,2048]{3,2,1,0:T(8,128)(2,1)} %get-tuple-element.208), kind=kLoop, calls=%fused_computation.67.clone.1 | loop fusion | bytes 37748736 | tf_op jit(solution)/shard_map/while/body/eval_jaxpr/slice | solution.py:73
  596.7 8.1 %fusion.62 = (bf16[1,2,1152,2048]{3,2,1,0:T(8,128)(2,1)S(1)}, bf16[1,2,1152,2048]{3,2,1,0:T(8,128)(2,1)S(1)}) fusion(bf16[2,2,1152,2048]{3,2,1,0:T(8,128)(2,1)} %get-tuple-element.208), kind=kLoop, calls=%fused_computation.67.clone.1 | loop fusion | bytes 37748736 | tf_op jit(solution)/shard_map/while/body/eval_jaxpr/slice | solution.py:73
  611.9 8.1 %fusion.62 = (bf16[1,2,1152,2048]{3,2,1,0:T(8,128)(2,1)S(1)}, bf16[1,2,1152,2048]{3,2,1,0:T(8,128)(2,1)S(1)}) fusion(bf16[2,2,1152,2048]{3,2,1,0:T(8,128)(2,1)} %get-tuple-element.208), kind=kLoop, calls=%fused_computation.67.clone.1 | loop fusion | bytes 37748736 | tf_op jit(solution)/shard_map/while/body/eval_jaxpr/slice | solution.py:73
  627.1 8.1 %fusion.62 = (bf16[1,2,1152,2048]{3,2,1,0:T(8,128)(2,1)S(1)}, bf16[1,2,1152,2048]{3,2,1,0:T(8,128)(2,1)S(1)}) fusion(bf16[2,2,1152,2048]{3,2,1,0:T(8,128)(2,1)} %get-tuple-element.208), kind=kLoop, calls=%fused_computation.67.clone.1 | loop fusion | bytes 37748736 | tf_op jit(solution)/shard_map/while/body/eval_jaxpr/slice | solution.py:73
  642.3 8.1 %fusion.62 = (bf16[1,2,1152,2048]{3,2,1,0:T(8,128)(2,1)S(1)}, bf16[1,2,1152,2048]{3,2,1,0:T(8,128)(2,1)S(1)}) fusion(bf16[2,2,1152,2048]{3,2,1,0:T(8,128)(2,1)} %get-tuple-element.208), kind=kLoop, calls=%fused_computation.67.clone.1 | loop fusion | bytes 37748736 | tf_op jit(solution)/shard_map/while/body/eval_jaxpr/slice | solution.py:73
  657.4 8.1 %fusion.62 = (bf16[1,2,1152,2048]{3,2,1,0:T(8,128)(2,1)S(1)}, bf16[1,2,1152,2048]{3,2,1,0:T(8,128)(2,1)S(1)}) fusion(bf16[2,2,1152,2048]{3,2,1,0:T(8,128)(2,1)} %get-tuple-element.208), kind=kLoop, calls=%fused_computation.67.clone.1 | loop fusion | bytes 37748736 | tf_op jit(solution)/shard_map/while/body/eval_jaxpr/slice | solution.py:73
  672.6 8.1 %fusion.62 = (bf16[1,2,1152,2048]{3,2,1,0:T(8,128)(2,1)S(1)}, bf16[1,2,1152,2048]{3,2,1,0:T(8,128)(2,1)S(1)}) fusion(bf16[2,2,1152,2048]{3,2,1,0:T(8,128)(2,1)} %get-tuple-element.208), kind=kLoop, calls=%fused_computation.67.clone.1 | loop fusion | bytes 37748736 | tf_op jit(solution)/shard_map/while/body/eval_jaxpr/slice | solution.py:73
  (214 shorter events, 131.4 us)
Async XLA Ops:
  12.0 9.3 %copy-start.1 = (bf16[2,1,128,2048]{3,2,1,0:T(8,128)(2,1)S(1)}, bf16[2,1,128,2048]{3,2,1,0:T(8,128)(2,1)}, u32[]{:S(2)}) copy-start(bf16[2,1,128,2048]{3,2,1,0:T(8,128)(2,1)} %param.9) | copy-start | bytes 3145732
  12.0 431.8 %all-to-all-start = ((bf16[16,128,2048]{2,1,0:T(8,128)(2,1)}), bf16[16,128,2048]{2,1,0:T(8,128)(2,1)}, u32[]{:S(2)}, u32[]{:S(2)}) async-start(bf16[16,128,2048]{2,1,0:T(8,128)(2,1)} %stack.135), calls=%async_computation | async-start | bytes 16777216 | tf_op jit(solution)/shard_map/all_to_all | solution.py:36
  20.5 181.3 %copy-start.3 = (s32[2,1,9]{2,1,0:T(1,128)S(1)}, s32[2,1,9]{2,1,0:T(1,128)}, u32[]{:S(2)}) copy-start(s32[2,1,9]{2,1,0:T(1,128)} %param.11) | copy-start | bytes 220
  20.5 423.3 %all-gather.2.cloned.1.call-start = ((), (), s32[]{:S(2)}) async-start(), calls=%async_computation.1 | async-start | bytes 8912896 | tf_op jit(solution)/shard_map/all_gather | solution.py:34
  22.7 168.7 %collective-permute-start = (bf16[2,1,1,128,2048]{4,3,0,2,1:T(8,128)(2,1)S(1)}, bf16[2,1,1,128,2048]{4,3,0,2,1:T(8,128)(2,1)S(1)}, u32[]{:S(2)}, u32[]{:S(2)}) collective-permute-start(bf16[2,1,1,128,2048]{4,3,0,2,1:T(8,128)(2,1)S(1)} %get-tuple-element.97), channel_id=1, source_target_pairs={{0,16},{16,32},{32,48},{48,64},{64,80},{80,96},{96,112},{112,128},... | collective-permute-start | bytes 3145736 | tf_op jit(solution)/shard_map/ppermute | solution.py:18
  24.6 166.8 %collective-permute-start.1 = (bf16[2,1,1,128,2048]{4,3,0,2,1:T(8,128)(2,1)S(1)}, bf16[2,1,1,128,2048]{4,3,0,2,1:T(8,128)(2,1)S(1)}, u32[]{:S(2)}, u32[]{:S(2)}) collective-permute-start(bf16[2,1,1,128,2048]{4,3,0,2,1:T(8,128)(2,1)S(1)} %get-tuple-element.98), channel_id=1, source_target_pairs={{16,0},{32,16},{48,32},{64,48},{80,64},{96,80},{112,96},{128,112},... | collective-permute-start | bytes 3145736 | tf_op jit(solution)/shard_map/ppermute | solution.py:20
  191.4 1.1 copy-start
  195.9 223.6 %collective-permute-start.2 = (bf16[2,4,1,128,2048]{4,3,0,2,1:T(8,128)(2,1)}, bf16[2,4,1,128,2048]{4,3,0,2,1:T(8,128)(2,1)}, u32[]{:S(2)}, u32[]{:S(2)}) collective-permute-start(bf16[2,4,1,128,2048]{4,3,0,2,1:T(8,128)(2,1)} %pad_maximum_fusion.1), channel_id=1, source_target_pairs={{0,1},{1,2},{2,3},{3,4},{4,5},{5,6},{6,7},{7,8},{8,9},{9,10},{10,1... | collective-permute-start | bytes 12582920 | tf_op jit(solution)/shard_map/ppermute | solution.py:18
  197.8 227.4 %collective-permute-start.3 = (bf16[2,4,1,128,2048]{4,3,0,2,1:T(8,128)(2,1)}, bf16[2,4,1,128,2048]{4,3,0,2,1:T(8,128)(2,1)}, u32[]{:S(2)}, u32[]{:S(2)}) collective-permute-start(bf16[2,4,1,128,2048]{4,3,0,2,1:T(8,128)(2,1)} %pad_maximum_fusion.1), channel_id=1, source_target_pairs={{1,0},{2,1},{3,2},{4,3},{5,4},{6,5},{7,6},{8,7},{9,8},{10,9},{11,1... | collective-permute-start | bytes 12582920 | tf_op jit(solution)/shard_map/ppermute | solution.py:20
  436.1 7.7 %copy-start.2 = (bf16[16,2,128,128]{3,2,1,0:T(8,128)(2,1)S(1)}, bf16[16,2,128,128]{3,2,1,0:T(8,128)(2,1)}, u32[]{:S(2)}) copy-start(bf16[16,2,128,128]{3,2,1,0:T(8,128)(2,1)} %custom-call.2) | copy-start | bytes 3145732
Sparse Core Ops, SparseCore 0:
  23.2 317.5 all-gather.1
